TPU v7x, 32 devices: a whole 2x2x4 slice. The times are simulated.
32 devices in a mesh: grp: 8 (over y, x, core), seq: 4 (over z).
Axes of the slice: x: 2, y: 2, z: 4, core: 2. Of those that a mesh axis runs over, the one named last changes fastest.
Arguments:
- tokens: bfloat16 [8192, 2048], P(('grp', 'seq')), may hold values from -6 to 6
- cotangent: bfloat16 [8192, 2048], P(('grp', 'seq')), may hold values from -6 to 6
- segment_ids: int32 [8192], P(('grp', 'seq')), may hold values from 0 to 31, never falling along the last dimension, each value on 1 to 768 neighbouring positions
- tile_owner_slots: int32 [166], replicated, may hold values from 0 to 167, as said below
- weights_low: bfloat16 [168, 2048, 128], P('grp', 'seq')
- master: float32 [168, 2048, 128], P('grp', 'seq')
- moment_one: float32 [168, 2048, 128], P('grp', 'seq')
- moment_two: float32 [168, 2048, 128], P('grp', 'seq'), as said below
- left_basis_set: float32 [168, 2048, 512], P('grp', 'seq'), as said below
- right_basis_set: float32 [168, 512, 128], P('grp', 'seq'), as said below
- gains: float32 [2, 2048], replicated, may hold values from 0.5 to 1.5
- gain_moment_one: float32 [2, 2048], replicated, may hold values from -28 to 28
- gain_moment_two: float32 [2, 2048], replicated, may hold values from 430.8992 to 1720.32
Outputs:
- block_out: bfloat16 [8192, 2048], P(('grp', 'seq'))
- input_grad: float32 [8192, 2048], P(('grp', 'seq'))
- new_master: float32 [168, 2048, 128], P('grp', 'seq')
- new_moment_one: float32 [168, 2048, 128], P('grp', 'seq')
- new_moment_two: float32 [168, 2048, 128], P('grp', 'seq')
- gain_grads: float32 [2, 2048], replicated
- new_gains: float32 [2, 2048], replicated
- new_gain_one: float32 [2, 2048], replicated
- new_gain_two: float32 [2, 2048], replicated
Inputs may be any that keep to these rules, and one draw needn't show every extreme that they name: `tile_owner_slots`: the entries are distinct; slot q belongs to data group q // 21. `segment_ids`: never falls along the tokens. `left_basis_set`: each 512 x 512 block is orthogonal. `right_basis_set`: each 128 x 128 block is orthogonal. `moment_two`: positive.
All inputs are finite; a program needn't handle non-finite values.
Results may differ from a plain program's by a relative error of at most 0.015.
Values may be sent and summed in bfloat16 or wider, within the bound.
A program may use at most 704 MiB of HBM per device.

v0:
```python
import jax
import jax.numpy as jnp
from jax import lax
from jax.sharding import PartitionSpec as P

MODEL_WIDTH = 2048
NH = 16
HD = 128
FF = 5632
SEQLEN = 1024
NORM_EPS = 1e-05
BETA_ONE = 0.95
BETA_TWO = 0.95
ADAM_EPS = 1e-08
WEIGHT_DECAY = 0.01
LEARN_RATE = 0.03
GAIN_RATE = 1.5
ROPE_BASE = 10000.0
MASKED = -1e30
PRECISE = lax.Precision.HIGHEST


def rotate(values, positions, direction):
    head_width = values.shape[-1]
    half_width = head_width // 2
    frequency = ROPE_BASE ** (-(jnp.arange(half_width, dtype=jnp.float32) * 2.0) / head_width)
    angles = positions.astype(jnp.float32)[:, None] * frequency[None, :]
    cosine = jnp.cos(angles)[:, None, :]
    sine_part = (jnp.sin(angles) * direction)[:, None, :]
    leading = values[..., :half_width]
    trailing = values[..., half_width:]
    return jnp.concatenate(
        [leading * cosine - trailing * sine_part, trailing * cosine + leading * sine_part], axis=-1
    )


def visible(query_index, key_index, query_seg, key_seg):
    causal = query_index[:, None] >= key_index[None, :]
    same_seq = query_index[:, None] // SEQLEN == key_index[None, :] // SEQLEN
    same_doc = query_seg[:, None] == key_seg[None, :]
    return causal & same_seq & same_doc


def contract(left_side, right_side):
    return lax.dot_general(
        left_side, right_side, (((0,), (0,)), ((), ())), preferred_element_type=jnp.float32
    )


def times_transpose(left_side, right_side):
    return lax.dot_general(
        left_side, right_side, (((1,), (1,)), ((), ())), preferred_element_type=jnp.float32
    )


def attend(queries, key_rows, value_rows, query_index, query_seg, key_index, key_seg):
    query_total, head_count, head_width = queries.shape
    block_rows = min(512, query_total)
    block_count = query_total // block_rows
    score_scale = head_width ** (-0.5)

    def one_block(inputs):
        block_queries, block_index, block_seg = inputs
        raw_scores = jnp.einsum(
            "qhd,kd->hqk", block_queries, key_rows, preferred_element_type=jnp.float32
        )
        allowed = visible(block_index, key_index, block_seg, key_seg)
        score_matrix = jnp.where(allowed[None], raw_scores * score_scale, MASKED)
        highest = jnp.max(score_matrix, axis=-1, keepdims=True)
        exponent = jnp.exp(score_matrix - highest)
        totals = jnp.sum(exponent, axis=-1, keepdims=True)
        probs_low = (exponent / totals).astype(jnp.bfloat16)
        context = jnp.einsum(
            "hqk,kd->qhd", probs_low, value_rows, preferred_element_type=jnp.float32
        )
        return (context, jnp.transpose((highest + jnp.log(totals))[..., 0]))

    context, log_totals = lax.map(
        one_block,
        (
            queries.reshape(block_count, block_rows, head_count, head_width),
            query_index.reshape(block_count, block_rows),
            query_seg.reshape(block_count, block_rows),
        ),
    )
    return (
        context.reshape(query_total, head_count, head_width),
        log_totals.reshape(query_total, head_count),
    )


def attend_back(
    queries, key_rows, value_rows, grads_low, log_totals, query_index, query_seg, key_index, key_seg
):
    query_total, head_count, head_width = queries.shape
    block_rows = min(512, query_total)
    block_count = query_total // block_rows
    score_scale = head_width ** (-0.5)

    def one_block(running, inputs):
        block_queries, block_grads, block_totals, block_index, block_seg = inputs
        raw_scores = jnp.einsum(
            "qhd,kd->hqk", block_queries, key_rows, preferred_element_type=jnp.float32
        )
        allowed = visible(block_index, key_index, block_seg, key_seg)
        shifted = raw_scores * score_scale - jnp.transpose(block_totals)[:, :, None]
        probs = jnp.where(allowed[None], jnp.exp(shifted), 0.0)
        prob_grad = jnp.einsum(
            "qhd,kd->hqk", block_grads, value_rows, preferred_element_type=jnp.float32
        )
        centre = jnp.sum(probs * prob_grad, axis=-1, keepdims=True)
        score_grad = (probs * (prob_grad - centre) * score_scale).astype(jnp.bfloat16)
        query_part = jnp.einsum(
            "hqk,kd->qhd", score_grad, key_rows, preferred_element_type=jnp.float32
        )
        key_part = running[0] + jnp.einsum(
            "hqk,qhd->kd", score_grad, block_queries, preferred_element_type=jnp.float32
        )
        value_part = running[1] + jnp.einsum(
            "hqk,qhd->kd",
            probs.astype(jnp.bfloat16),
            block_grads,
            preferred_element_type=jnp.float32,
        )
        return ((key_part, value_part), query_part)

    zeros_rows = jnp.zeros(key_rows.shape, jnp.float32)
    (key_grad, value_grad), query_grad = lax.scan(
        one_block,
        (zeros_rows, zeros_rows),
        (
            queries.reshape(block_count, block_rows, head_count, head_width),
            grads_low.reshape(block_count, block_rows, head_count, head_width),
            log_totals.reshape(block_count, block_rows, head_count),
            query_index.reshape(block_count, block_rows),
            query_seg.reshape(block_count, block_rows),
        ),
    )
    return (query_grad.reshape(query_total, head_count, head_width), key_grad, value_grad)


def local(
    tokens,
    cotangent,
    segment_ids,
    tile_owner_slots,
    weights_low,
    master,
    moment_one,
    moment_two,
    left_basis_set,
    right_basis_set,
    gains,
    gain_moment_one,
    gain_moment_two,
):
    grp_count = lax.axis_size("grp")
    seq_count = lax.axis_size("seq")
    grp_here = lax.axis_index("grp")
    rows_here = tokens.shape[0]
    slots_here, rows_block, tile_width = weights_low.shape
    query_cols = NH * HD
    value_end = query_cols + 2 * HD
    output_end = value_end + MODEL_WIDTH
    attn_tiles = output_end // tile_width
    hidden_tiles = FF // tile_width
    share = -(-hidden_tiles // grp_count)
    share_cols = share * tile_width
    sub_rows = rows_block // grp_count
    local_index = lax.axis_index("seq") * rows_here + jnp.arange(rows_here, dtype=jnp.int32)
    local_place = local_index % SEQLEN
    plane_tiles = lax.all_gather(weights_low, "grp", axis=0, tiled=True)
    hidden_ids = grp_here * share + jnp.arange(share, dtype=jnp.int32)
    real = hidden_ids < hidden_tiles
    hidden_ids = jnp.minimum(hidden_ids, hidden_tiles - 1)
    feed_ids = (
        attn_tiles + jnp.arange(3, dtype=jnp.int32)[:, None] * hidden_tiles + hidden_ids[None, :]
    ).reshape(-1)
    attn_rows = lax.dynamic_slice_in_dim(plane_tiles, grp_here * sub_rows, sub_rows, axis=1)
    attn_rows = jnp.transpose(attn_rows[tile_owner_slots[:attn_tiles]], (1, 0, 2)).reshape(
        sub_rows, output_end
    )
    attn_weights = lax.all_gather(attn_rows, "seq", axis=0, tiled=False)
    attn_weights = lax.all_gather(attn_weights, "grp", axis=1, tiled=True).reshape(
        MODEL_WIDTH, output_end
    )
    feed_tiles = jnp.where(
        jnp.tile(real, 3)[:, None, None], plane_tiles[tile_owner_slots[feed_ids]], 0
    )
    feed_rows = jnp.transpose(feed_tiles, (1, 0, 2)).reshape(rows_block, 3 * share_cols)
    feed_weights = lax.all_gather(feed_rows, "seq", axis=0, tiled=True)
    cot_plane = lax.all_gather(cotangent, "grp", axis=0, tiled=True)
    tok_float = tokens.astype(jnp.float32)
    inverse_one = lax.rsqrt(jnp.mean(tok_float * tok_float, axis=-1, keepdims=True) + NORM_EPS)
    normed = (tok_float * inverse_one * gains[0]).astype(jnp.bfloat16)
    projected = jnp.dot(normed, attn_weights[:, :value_end], preferred_element_type=jnp.float32)
    queries = rotate(projected[:, :query_cols].reshape(rows_here, NH, HD), local_place, 1.0).astype(
        jnp.bfloat16
    )
    key_rows = (
        rotate(
            projected[:, query_cols : query_cols + HD].reshape(rows_here, 1, HD), local_place, 1.0
        )
        .reshape(rows_here, HD)
        .astype(jnp.bfloat16)
    )
    value_rows = projected[:, query_cols + HD : value_end].astype(jnp.bfloat16)
    all_pairs = lax.all_gather(
        jnp.concatenate([key_rows, value_rows], axis=1), "seq", axis=0, tiled=True
    )
    all_keys = all_pairs[:, :HD]
    all_values = all_pairs[:, HD:]
    all_segs = lax.all_gather(segment_ids, "seq", axis=0, tiled=True)
    group_index = jnp.arange(all_keys.shape[0], dtype=jnp.int32)
    group_place = group_index % SEQLEN
    heads_here = NH // seq_count
    head_queries = lax.all_to_all(
        queries.reshape(rows_here, query_cols), "seq", split_axis=1, concat_axis=0, tiled=True
    ).reshape(-1, heads_here, HD)
    head_context, log_totals = attend(
        head_queries, all_keys, all_values, group_index, all_segs, group_index, all_segs
    )
    context = lax.all_to_all(
        head_context.reshape(-1, heads_here * HD).astype(jnp.bfloat16),
        "seq",
        split_axis=0,
        concat_axis=1,
        tiled=True,
    )
    branch = jnp.dot(context, attn_weights[:, value_end:], preferred_element_type=jnp.float32)
    hidden = tok_float + branch
    inverse_two = lax.rsqrt(jnp.mean(hidden * hidden, axis=-1, keepdims=True) + NORM_EPS)
    normed_two = (hidden * inverse_two * gains[1]).astype(jnp.bfloat16)
    normed_plane = lax.all_gather(normed_two, "grp", axis=0, tiled=True)
    gating_weights = feed_weights[:, : 2 * share_cols]
    down_weights = feed_weights[:, 2 * share_cols :]
    gate_up = jnp.dot(normed_plane, gating_weights, preferred_element_type=jnp.float32)
    gate = gate_up[:, :share_cols]
    upper = gate_up[:, share_cols:]
    sigmoid_gate = jax.nn.sigmoid(gate)
    silu_gate = jax.nn.silu(gate)
    activated = (silu_gate * upper).astype(jnp.bfloat16)
    act_grad = jnp.dot(cot_plane, down_weights, preferred_element_type=jnp.float32)
    gate_grad = (act_grad * upper * sigmoid_gate * (1.0 + gate * (1.0 - sigmoid_gate))).astype(
        jnp.bfloat16
    )
    up_grad = (act_grad * silu_gate).astype(jnp.bfloat16)
    gating_grad = jnp.concatenate([gate_grad, up_grad], axis=1)
    norm_two_grad = lax.psum_scatter(
        times_transpose(gating_grad, gating_weights).astype(jnp.bfloat16),
        "grp",
        scatter_dimension=0,
        tiled=True,
    ).astype(jnp.float32)
    feed_grads = jnp.concatenate(
        [contract(normed_plane, gating_grad), contract(cot_plane, activated)], axis=1
    ).astype(jnp.bfloat16)
    feed_grads = lax.psum_scatter(feed_grads, "seq", scatter_dimension=0, tiled=True)
    feed_grads = jnp.transpose(feed_grads.reshape(rows_block, 3 * share, tile_width), (1, 0, 2))
    feed_grads = lax.all_gather(feed_grads, "grp", axis=0, tiled=True)
    feed_out = lax.psum_scatter(
        times_transpose(activated, down_weights).astype(jnp.bfloat16),
        "grp",
        scatter_dimension=0,
        tiled=True,
    ).astype(jnp.float32)
    block_out = (hidden + feed_out).astype(jnp.bfloat16)
    out_grad = cotangent.astype(jnp.float32)
    gain_two_term = jnp.sum(norm_two_grad * hidden * inverse_two, axis=0)
    hidden_grad = (
        out_grad
        + inverse_two * gains[1] * norm_two_grad
        - hidden
        * inverse_two**3
        * jnp.mean(hidden * gains[1] * norm_two_grad, axis=-1, keepdims=True)
    )
    branch_grad = hidden_grad.astype(jnp.bfloat16)
    context_grad = times_transpose(branch_grad, attn_weights[:, value_end:]).astype(jnp.bfloat16)
    head_grads = lax.all_to_all(
        context_grad, "seq", split_axis=1, concat_axis=0, tiled=True
    ).reshape(-1, heads_here, HD)

    def reduce_rows(part):
        cols = part.shape[1]
        blocks = jnp.transpose(
            part.astype(jnp.bfloat16).reshape(seq_count, grp_count, sub_rows, cols), (1, 0, 2, 3)
        ).reshape(grp_count * seq_count * sub_rows, cols)
        summed = lax.psum_scatter(blocks, ("grp", "seq"), scatter_dimension=0, tiled=True)
        return lax.all_gather(summed, "grp", axis=0, tiled=True)

    out_grads = reduce_rows(contract(context, branch_grad))
    head_query_grad, key_part, value_part = attend_back(
        head_queries,
        all_keys,
        all_values,
        head_grads,
        log_totals,
        group_index,
        all_segs,
        group_index,
        all_segs,
    )
    turned_query = (
        rotate(head_query_grad, group_place, -1.0).reshape(-1, heads_here * HD).astype(jnp.bfloat16)
    )
    query_grad = lax.all_to_all(turned_query, "seq", split_axis=0, concat_axis=1, tiled=True)
    key_part = rotate(key_part[:, None, :], group_place, -1.0)[:, 0, :]
    pair_grad = lax.psum_scatter(
        jnp.concatenate([key_part, value_part], axis=1), "seq", scatter_dimension=0, tiled=True
    )
    projected_grad = jnp.concatenate([query_grad, pair_grad.astype(jnp.bfloat16)], axis=1)
    in_grads = reduce_rows(contract(normed, projected_grad))
    norm_one_grad = times_transpose(projected_grad, attn_weights[:, :value_end])
    gain_one_term = jnp.sum(norm_one_grad * tok_float * inverse_one, axis=0)
    input_grad = (
        hidden_grad
        + inverse_one * gains[0] * norm_one_grad
        - tok_float
        * inverse_one**3
        * jnp.mean(tok_float * gains[0] * norm_one_grad, axis=-1, keepdims=True)
    )
    gain_grads = lax.psum(jnp.stack([gain_one_term, gain_two_term]), ("grp", "seq"))
    tile_count = tile_owner_slots.shape[0]
    tile_of_slot = (
        jnp.full((grp_count * slots_here,), tile_count, jnp.int32)
        .at[tile_owner_slots]
        .set(jnp.arange(tile_count, dtype=jnp.int32))
    )
    tiles_here = lax.dynamic_slice_in_dim(tile_of_slot, grp_here * slots_here, slots_here)
    attn_grads = jnp.transpose(
        jnp.concatenate([in_grads, out_grads], axis=1).reshape(rows_block, attn_tiles, tile_width),
        (1, 0, 2),
    )
    feed_at = jnp.clip(tiles_here - attn_tiles, 0, 3 * hidden_tiles - 1)
    which, column = (feed_at // hidden_tiles, feed_at % hidden_tiles)
    feed_at = column // share * (3 * share) + which * share + column % share
    picked = jnp.where(
        (tiles_here < attn_tiles)[:, None, None],
        attn_grads[jnp.minimum(tiles_here, attn_tiles - 1)],
        feed_grads[feed_at],
    )
    reduced_sum = jnp.where((tiles_here < tile_count)[:, None, None], picked, 0).astype(jnp.float32)
    turned = jnp.einsum("zji,zjc->zic", left_basis_set, reduced_sum)
    turned = jnp.einsum("zic,zcd->zid", turned, right_basis_set)
    new_one = BETA_ONE * moment_one + (1.0 - BETA_ONE) * turned
    new_two = BETA_TWO * moment_two + (1.0 - BETA_TWO) * turned * turned
    scaled = new_one / (jnp.sqrt(new_two) + ADAM_EPS)
    restored = jnp.einsum("zij,zjd->zid", left_basis_set, scaled)
    restored = jnp.einsum("zid,zed->zie", restored, right_basis_set)
    new_master = master * (1.0 - LEARN_RATE * WEIGHT_DECAY) - LEARN_RATE * restored
    gain_one = BETA_ONE * gain_moment_one + (1.0 - BETA_ONE) * gain_grads
    gain_two = BETA_TWO * gain_moment_two + (1.0 - BETA_TWO) * gain_grads * gain_grads
    new_gains = gains - GAIN_RATE * gain_one / (jnp.sqrt(gain_two) + ADAM_EPS)
    return (
        block_out,
        input_grad,
        new_master,
        new_one,
        new_two,
        gain_grads,
        new_gains,
        gain_one,
        gain_two,
    )


def solution(mesh):
    return jax.shard_map(
        local,
        mesh=mesh,
        in_specs=(
            P(("grp", "seq"), None),
            P(("grp", "seq"), None),
            P(("grp", "seq")),
            P(),
            P("grp", "seq", None),
            P("grp", "seq", None),
            P("grp", "seq", None),
            P("grp", "seq", None),
            P("grp", "seq", None),
            P("grp", "seq", None),
            P(),
            P(),
            P(),
        ),
        out_specs=(
            P(("grp", "seq"), None),
            P(("grp", "seq"), None),
            P("grp", "seq", None),
            P("grp", "seq", None),
            P("grp", "seq", None),
            P(),
            P(),
            P(),
            P(),
        ),
        check_vma=False,
    )
```

profile of v0, /device:TPU:0, one launch (start us, length us, event | category | flops | bytes accessed | tf_op | source)
XLA Modules:
  0.0 1731.6 jit_solution(6610942294189539147)
XLA Ops:
  8.7 116.0 %all-gather.11.cloned.1.call-done = bf16[168,512,128]{2,1,0:T(8,128)(2,1)} async-done(((bf16[21,512,128]{2,1,0:T(8,128)(2,1)}), bf16[168,512,128]{2,1,0:T(8,128)(2,1)}) %all-gather.11.cloned.1.call-update) | async-done | bytes 22020112 | tf_op jit(solution)/shard_map/all_gather | solution.py:172
  134.4 48.4 %all-gather.13.cloned.1.call-done = bf16[4,64,4352]{2,1,0:T(8,128)(2,1)} async-done(((bf16[1,64,4352]{2,1,0:T(8,128)(2,1)}), bf16[4,64,4352]{2,1,0:T(8,128)(2,1)}) %all-gather.13.cloned.1.call-update) | async-done | bytes 2228240 | tf_op jit(solution)/shard_map/all_gather | solution.py:183
  204.3 73.6 %all-gather.15.cloned.1.call-done = bf16[4,512,4352]{2,1,0:T(8,128)(2,1)} async-done(((bf16[4,64,4352]{2,1,0:T(8,128)(2,1)}), bf16[4,512,4352]{2,1,0:T(8,128)(2,1)}) %all-gather.15.cloned.1.call-update) | async-done | bytes 17825808 | tf_op jit(solution)/shard_map/all_gather | solution.py:184
  296.3 40.8 %all-gather = s32[4,1,256]{2,1,0:T(1,128)S(1)} all-gather(s32[1,1,256]{2,1,0:T(1,128)} %bitcast.336), channel_id=1, replica_groups=mesh['grp'=8,'seq'=4] {'seq'}, dimensions={0}, use_global_device_ids=true | all-gather | bytes 5120 | tf_op jit(solution)/shard_map/all_gather | solution.py:213
  339.6 43.2 %all_gather.37 = bf16[1024,256]{0,1:T(8,128)(2,1)S(1)} all-gather(bf16[256,256]{0,1:T(8,128)(2,1)S(1)} %pad_maximum_fusion.11), channel_id=1, replica_groups=mesh['grp'=8,'seq'=4] {'seq'}, dimensions={0}, use_global_device_ids=true | all-gather | bytes 655360 | tf_op jit(solution)/shard_map/all_gather | solution.py:208
  388.0 17.3 while.36
  410.6 59.3 %all_to_all.61 = bf16[4,256,512]{2,1,0:T(8,128)(2,1)} all-to-all(bf16[4,256,512]{2,1,0:T(8,128)(2,1)} %convert_element_type.137), channel_id=1, replica_groups=mesh['grp'=8,'seq'=4] {'seq'}, dimensions={0} | all-to-all | bytes 2097152 | tf_op jit(solution)/shard_map/all_to_all | solution.py:223
  481.9 18.0 %all-gather.19.cloned.1.call-done = bf16[2048,2304]{0,1:T(8,128)(2,1)} async-done(((bf16[512,2304]{0,1:T(8,128)(2,1)}), bf16[2048,2304]{0,1:T(8,128)(2,1)}) %all-gather.19.cloned.1.call-update) | async-done | bytes 9437200 | tf_op jit(solution)/shard_map/all_gather | solution.py:191
  499.8 54.9 %all-gather.17.cloned.1.call-done = bf16[2048,2048]{1,0:T(8,128)(2,1)} async-done(((bf16[256,2048]{1,0:T(8,128)(2,1)}), bf16[2048,2048]{1,0:T(8,128)(2,1)}) %all-gather.17.cloned.1.call-update) | async-done | bytes 8388624 | tf_op jit(solution)/shard_map/all_gather | solution.py:234
  554.8 19.0 %fusion.95 = f32[2048,1536]{0,1:T(8,128)} fusion(bf16[2048,2048]{1,0:T(8,128)(2,1)} %all-gather.17.cloned.1.call-done, bf16[2048,2304]{0,1:T(8,128)(2,1)} %all-gather.19.cloned.1.call-done), kind=kOutput, calls=%fused_computation.134 | convolution fusion | flops 12884901888 | bytes 27262976 | tf_op jit(solution)/shard_map/dot_general | solution.py:237
  573.7 37.2 %all-gather.21.cloned.1.call-done = bf16[2048,2048]{1,0:T(8,128)(2,1)} async-done(((bf16[256,2048]{1,0:T(8,128)(2,1)}), bf16[2048,2048]{1,0:T(8,128)(2,1)}) %all-gather.21.cloned.1.call-update) | async-done | bytes 8388624 | tf_op jit(solution)/shard_map/all_gather | solution.py:192
  610.9 16.7 fusion.91
  629.3 18.7 %convolution_convert_fusion.3 = bf16[2048,2048]{1,0:T(8,128)(2,1)} fusion(bf16[2048,2304]{0,1:T(8,128)(2,1)} %all-gather.19.cloned.1.call-done, bf16[2048,768]{0,1:T(8,128)(2,1)} %get-tuple-element.680, bf16[2048,768]{0,1:T(8,128)(2,1)S(1)} %get-tuple-element.679), kind=kOutput, calls=%fused_computation.117 | convolution fusion | flops 12901679104 | bytes 20971520 | tf_op jit(solution)/shard_map/dot_general | solution.py:51
  648.1 11.9 convolution_convert_fusion.4
  660.0 59.5 %reduce-scatter.9.cloned.1.call-done = bf16[256,2048]{1,0:T(8,128)(2,1)} async-done(((bf16[2048,2048]{1,0:T(8,128)(2,1)}), bf16[256,2048]{1,0:T(8,128)(2,1)}) %reduce-scatter.9.cloned.1.call-update) | async-done | bytes 1048592 | tf_op jit(solution)/shard_map/reduce_scatter | solution.py:249
  722.5 72.2 %reduce-scatter.7.cloned.1.call-done = bf16[256,2048]{1,0:T(8,128)(2,1)} async-done(((bf16[2048,2048]{1,0:T(8,128)(2,1)}), bf16[256,2048]{1,0:T(8,128)(2,1)}) %reduce-scatter.7.cloned.1.call-update) | async-done | bytes 1048592 | tf_op jit(solution)/shard_map/reduce_scatter | solution.py:261
  811.1 25.8 %all-to-all-done.2 = bf16[256,4,512]{2,0,1:T(8,128)(2,1)} async-done(((bf16[256,4,512]{2,0,1:T(8,128)(2,1)}), bf16[256,4,512]{2,0,1:T(8,128)(2,1)}, u32[]{:S(2)}, u32[]{:S(2)}) %all-to-all-start.2) | async-done | bytes 1048608 | tf_op jit(solution)/shard_map/all_to_all | solution.py:279
  839.5 123.5 %while.37 = (s32[]{:T(128)}, f32[1024,128]{1,0:T(8,128)}, f32[1024,128]{1,0:T(8,128)}, f32[2,512,4,128]{3,1,0,2:T(8,128)}, s32[2,512]{1,0:T(2,128)S(1)}, /*index...) while((s32[]{:T(128)}, f32[1024,128]{1,0:T(8,128)}, ...), condition=%wide.region_11.12_spmd.clone.clone, body=%wide.region_9.11_spmd.clone.clone.sunk | while | flops 2742048256 | bytes 106783928 | solution.py:128
  850.3 22.8 %fusion.228 = f32[2,512,4,128]{3,1,0,2:T(8,128)} fusion(f32[2,512,4,128]{3,1,0,2:T(8,128)} %get-tuple-element.900, s32[]{:T(128)} %get-tuple-element.897, f32[512,4,1024]{2,0,1:T(8,128)} %fusion.223, f32[512,4,1024]{2,0,1:T(8,128)} %fusion.224, f32[4,512]{1,0:T(4,128)S(1)} %dynamic-slice_bitcast_fusion.2, pred[512,1024]{1,0:T(8,128)(4,1)} %fusion.225, ...), kind=kOutput, calls=%fused_computation.67.clone.1 | convolution fusion | flops 559942656 | bytes 35930624 | tf_op jit(solution)/shard_map/while/body/eval_jaxpr/hqk,kd->qhd/dot_general | solution.py:113
  873.1 21.3 %fusion.226 = f32[1024,128]{1,0:T(8,128)} fusion(f32[512,4,1024]{2,0,1:T(8,128)} %fusion.223, f32[512,4,1024]{2,0,1:T(8,128)} %fusion.224, f32[4,512]{1,0:T(4,128)S(1)} %dynamic-slice_bitcast_fusion.2, pred[512,1024]{1,0:T(8,128)(4,1)} %fusion.225, f32[1024,128]{1,0:T(8,128)} %get-tuple-element.898, ...), kind=kOutput, calls=%fused_computation.70.clone.1 | convolution fusion | flops 560204800 | bytes 36192768 | tf_op jit(solution)/shard_map/while/body/eval_jaxpr/hqk,qhd->kd/dot_general | solution.py:116
  912.0 22.8 %fusion.228 = f32[2,512,4,128]{3,1,0,2:T(8,128)} fusion(f32[2,512,4,128]{3,1,0,2:T(8,128)} %get-tuple-element.900, s32[]{:T(128)} %get-tuple-element.897, f32[512,4,1024]{2,0,1:T(8,128)} %fusion.223, f32[512,4,1024]{2,0,1:T(8,128)} %fusion.224, f32[4,512]{1,0:T(4,128)S(1)} %dynamic-slice_bitcast_fusion.2, pred[512,1024]{1,0:T(8,128)(4,1)} %fusion.225, ...), kind=kOutput, calls=%fused_computation.67.clone.1 | convolution fusion | flops 559942656 | bytes 35930624 | tf_op jit(solution)/shard_map/while/body/eval_jaxpr/hqk,kd->qhd/dot_general | solution.py:113
  934.8 21.3 %fusion.226 = f32[1024,128]{1,0:T(8,128)} fusion(f32[512,4,1024]{2,0,1:T(8,128)} %fusion.223, f32[512,4,1024]{2,0,1:T(8,128)} %fusion.224, f32[4,512]{1,0:T(4,128)S(1)} %dynamic-slice_bitcast_fusion.2, pred[512,1024]{1,0:T(8,128)(4,1)} %fusion.225, f32[1024,128]{1,0:T(8,128)} %get-tuple-element.898, ...), kind=kOutput, calls=%fused_computation.70.clone.1 | convolution fusion | flops 560204800 | bytes 36192768 | tf_op jit(solution)/shard_map/while/body/eval_jaxpr/hqk,qhd->kd/dot_general | solution.py:116
  977.2 41.2 %all_to_all.62 = bf16[4,256,512]{2,1,0:T(8,128)(2,1)} all-to-all(bf16[4,256,512]{2,1,0:T(8,128)(2,1)} %convert_element_type.151), channel_id=1, replica_groups=mesh['grp'=8,'seq'=4] {'seq'}, dimensions={0} | all-to-all | bytes 2097152 | tf_op jit(solution)/shard_map/all_to_all | solution.py:306
  1062.7 15.9 convolution_convert_fusion.1
  1078.6 11.5 pad_maximum_fusion
  1090.2 79.3 %reduce-scatter.13.cloned.1.call-done = bf16[64,2304]{1,0:T(8,128)(2,1)} async-done(((bf16[2048,2304]{1,0:T(8,128)(2,1)}), bf16[64,2304]{1,0:T(8,128)(2,1)}) %reduce-scatter.13.cloned.1.call-update) | async-done | bytes 294928 | tf_op jit(solution)/shard_map/reduce_scatter | solution.py:288
  1169.6 187.0 %reduce-scatter.15.cloned.1.call-done = bf16[64,2048]{1,0:T(8,128)(2,1)} async-done(((bf16[2048,2048]{1,0:T(8,128)(2,1)}), bf16[64,2048]{1,0:T(8,128)(2,1)}) %reduce-scatter.15.cloned.1.call-update) | async-done | bytes 262160 | tf_op jit(solution)/shard_map/reduce_scatter | solution.py:288
  1356.7 161.1 %reduce-scatter.17.cloned.1.call-done = bf16[512,2304]{0,1:T(8,128)(2,1)} async-done(((bf16[2048,2304]{0,1:T(8,128)(2,1)}), bf16[512,2304]{0,1:T(8,128)(2,1)}) %reduce-scatter.17.cloned.1.call-update) | async-done | bytes 2359312 | tf_op jit(solution)/shard_map/reduce_scatter | solution.py:258
  1534.5 41.6 %psum.7 = f32[2,2048]{1,0:T(2,128)S(1)} all-reduce(f32[2,2048]{1,0:T(2,128)S(1)} %pad_maximum_fusion.12), channel_id=1, replica_groups=mesh['grp'=8,'seq'=4] {'grp','seq'}, use_global_device_ids=true, to_apply=%region_20.21 | all-reduce | flops 4096 | bytes 32768 | tf_op jit(solution)/shard_map/psum | solution.py:322
  1605.0 76.1 %all-gather.27.cloned.1.call-done = bf16[144,512,128]{2,1,0:T(8,128)(2,1)} async-done(((bf16[18,512,128]{2,1,0:T(8,128)(2,1)}), bf16[144,512,128]{2,1,0:T(8,128)(2,1)}) %all-gather.27.cloned.1.call-update) | async-done | bytes 18874384 | tf_op jit(solution)/shard_map/all_gather | solution.py:260
  1690.0 18.5 %fusion.97 = (f32[21,512,128]{2,1,0:T(8,128)}, f32[21,512,128]{2,1,0:T(8,128)}) fusion(f32[21,512,128]{2,1,0:T(8,128)} %param.24, f32[21,512,128]{2,1,0:T(8,128)} %param.23, f32[21,128,128]{2,1,0:T(8,128)S(1)} %copy-done, f32[21,512,512]{2,1,0:T(8,128)} %param.25, bf16[21,512,128]{2,1,0:T(8,128)(2,1)} %gather_fusion.3, ...), kind=kOutput, calls=%fused_computation.136 | convolution fusion | flops 1772617728 | bytes 50921512 | tf_op jit(solution)/shard_map/zic,zcd->zid/dot_general | solution.py:344
  1708.5 16.1 multiply_subtract_fusion
  (235 shorter events, 264.9 us)
Async XLA Ops:
  7.2 1682.9 %copy-start = (f32[21,128,128]{2,1,0:T(8,128)S(1)}, f32[21,128,128]{2,1,0:T(8,128)}, u32[]{:S(2)}) copy-start(f32[21,128,128]{2,1,0:T(8,128)} %param.26) | copy-start | bytes 4128772
  7.2 117.5 %all-gather.11.cloned.1.call-start = ((), (), s32[]{:S(2)}) async-start(), calls=%async_computation.10 | async-start | bytes 24772608 | tf_op jit(solution)/shard_map/all_gather | solution.py:172
  7.9 174.9 %all-gather.13.cloned.1.call-start = ((), (), s32[]{:S(2)}) async-start(), calls=%async_computation.11 | async-start | bytes 2785280 | tf_op jit(solution)/shard_map/all_gather | solution.py:183
  8.7 174.4 %copy-start.1 = (s32[166]{0:T(256)S(1)}, s32[166]{0:T(256)}, u32[]{:S(2)}) copy-start(s32[166]{0:T(256)} %param.20) | copy-start | bytes 1996
  8.7 175.3 %copy-start.7 = (bf16[256,2048]{1,0:T(8,128)(2,1)S(1)}, bf16[256,2048]{1,0:T(8,128)(2,1)}, u32[]{:S(2)}) copy-start(bf16[256,2048]{1,0:T(8,128)(2,1)} %param.17) | copy-start | bytes 3145732
  134.4 143.5 %all-gather.15.cloned.1.call-start = ((), (), s32[]{:S(2)}) async-start(), calls=%async_computation.12 | async-start | bytes 20054016 | tf_op jit(solution)/shard_map/all_gather | solution.py:184
  182.9 317.0 %all-gather.19.cloned.1.call-start = ((), (), s32[]{:S(2)}) async-start(), calls=%async_computation.14 | async-start | bytes 11796480 | tf_op jit(solution)/shard_map/all_gather | solution.py:191
  202.7 136.5 %copy-start.22 = (f32[64]{0:T(128)}, f32[64]{0:T(128)S(1)}, u32[]{:S(2)}) copy-start(f32[64]{0:T(128)S(1)} %multiply_power_fusion) | copy-start | bytes 772
  203.3 80.9 %copy-start.19 = (f32[256]{0:T(256)}, f32[256]{0:T(256)S(1)}, u32[]{:S(2)}) copy-start(f32[256]{0:T(256)S(1)} %get-tuple-element.703) | copy-start | bytes 3076
  204.3 80.0 %copy-start.13 = (f32[1,2048]{1,0:T(1,128)}, f32[1,2048]{1,0:T(1,128)S(1)}, u32[]{:S(2)}) copy-start(f32[1,2048]{1,0:T(1,128)S(1)} %get-tuple-element.697) | copy-start | bytes 24580
  291.7 91.5 %all-to-all-start = ((bf16[256,4,512]{0,2,1:T(8,128)(2,1)}), bf16[256,4,512]{0,2,1:T(8,128)(2,1)S(1)}, u32[]{:S(2)}, u32[]{:S(2)}) async-start(bf16[256,4,512]{0,2,1:T(8,128)(2,1)} %bitcast.5), calls=%async_computation | async-start | bytes 2097152 | tf_op jit(solution)/shard_map/all_to_all | solution.py:217
  296.3 258.4 %all-gather.17.cloned.1.call-start = ((), (), s32[]{:S(2)}) async-start(), calls=%async_computation.13 | async-start | bytes 9437184 | tf_op jit(solution)/shard_map/all_gather | solution.py:234
  481.1 129.9 %all-gather.21.cloned.1.call-start = ((), (), s32[]{:S(2)}) async-start(), calls=%async_computation.16 | async-start | bytes 9437184 | tf_op jit(solution)/shard_map/all_gather | solution.py:192
  481.7 237.9 %reduce-scatter.9.cloned.1.call-start = ((), (), s32[]{:S(2)}) async-start(), calls=%async_computation.17 | async-start | bytes 9437184 | tf_op jit(solution)/shard_map/reduce_scatter | solution.py:249
  648.1 146.6 %reduce-scatter.7.cloned.1.call-start = ((), (), s32[]{:S(2)}) async-start(), calls=%async_computation.15 | async-start | bytes 9437184 | tf_op jit(solution)/shard_map/reduce_scatter | solution.py:261
  806.5 30.4 %all-to-all-start.2 = ((bf16[256,4,512]{2,0,1:T(8,128)(2,1)}), bf16[256,4,512]{2,0,1:T(8,128)(2,1)}, u32[]{:S(2)}, u32[]{:S(2)}) async-start(bf16[256,4,512]{2,0,1:T(8,128)(2,1)} %bitcast.312), calls=%async_computation.4 | async-start | bytes 2097152 | tf_op jit(solution)/shard_map/all_to_all | solution.py:279
  811.1 208.7 %reduce-scatter.11.cloned.1.call-start = ((), (), s32[]{:S(2)}) async-start(), calls=%async_computation.18 | async-start | bytes 1310720 | tf_op jit(solution)/shard_map/reduce_scatter | solution.py:308
  839.5 127.7 %copy-start.23 = (f32[64]{0:T(128)S(1)}, f32[64]{0:T(128)}, u32[]{:S(2)}) copy-start(f32[64]{0:T(128)} %copy-done.22) | copy-start | bytes 772
  971.8 197.8 %reduce-scatter.13.cloned.1.call-start = ((), (), s32[]{:S(2)}) async-start(), calls=%async_computation.19 | async-start | bytes 9732096 | tf_op jit(solution)/shard_map/reduce_scatter | solution.py:288
  974.5 46.6 %copy-start.8 = (bf16[256,2048]{1,0:T(8,128)(2,1)S(1)}, bf16[256,2048]{1,0:T(8,128)(2,1)}, u32[]{:S(2)}) copy-start(bf16[256,2048]{1,0:T(8,128)(2,1)} %param.17) | copy-start | bytes 3145732
  974.5 46.6 %copy-start.14 = (f32[1,2048]{1,0:T(1,128)S(1)}, f32[1,2048]{1,0:T(1,128)}, u32[]{:S(2)}) copy-start(f32[1,2048]{1,0:T(1,128)} %copy-done.13) | copy-start | bytes 24580
  974.5 46.6 %copy-start.20 = (f32[256]{0:T(256)S(1)}, f32[256]{0:T(256)}, u32[]{:S(2)}) copy-start(f32[256]{0:T(256)} %copy-done.19) | copy-start | bytes 3076
  1034.7 321.9 %reduce-scatter.15.cloned.1.call-start = ((), (), s32[]{:S(2)}) async-start(), calls=%async_computation.21 | async-start | bytes 8650752 | tf_op jit(solution)/shard_map/reduce_scatter | solution.py:288
  1051.9 465.9 %reduce-scatter.17.cloned.1.call-start = ((), (), s32[]{:S(2)}) async-start(), calls=%async_computation.23 | async-start | bytes 11796480 | tf_op jit(solution)/shard_map/reduce_scatter | solution.py:258
  1090.1 432.0 %copy-start.2 = (s32[166]{0:T(256)S(1)}, s32[166]{0:T(256)}, u32[]{:S(2)}) copy-start(s32[166]{0:T(256)} %param.20) | copy-start | bytes 1996
  1090.2 491.9 %all-gather.23.cloned.1.call-start = ((), (), s32[]{:S(2)}) async-start(), calls=%async_computation.20 | async-start | bytes 2654208 | tf_op jit(solution)/shard_map/all_gather | solution.py:289
  1169.5 412.5 %all-gather.25.cloned.1.call-start = ((), (), s32[]{:S(2)}) async-start(), calls=%async_computation.22 | async-start | bytes 2359296 | tf_op jit(solution)/shard_map/all_gather | solution.py:289
  1356.6 324.5 %all-gather.27.cloned.1.call-start = ((), (), s32[]{:S(2)}) async-start(), calls=%async_computation.24 | async-start | bytes 21233664 | tf_op jit(solution)/shard_map/all_gather | solution.py:260
  1525.1 51.6 %copy-start.16 = (f32[2,2048]{1,0:T(2,128)S(1)}, f32[2,2048]{1,0:T(2,128)}, u32[]{:S(2)}) copy-start(f32[2,2048]{1,0:T(2,128)} %param.27) | copy-start | bytes 49156
  1525.1 51.6 %copy-start.21 = (f32[2,2048]{1,0:T(2,128)S(1)}, f32[2,2048]{1,0:T(2,128)}, u32[]{:S(2)}) copy-start(f32[2,2048]{1,0:T(2,128)} %param.28) | copy-start | bytes 49156
  1600.1 90.0 %copy-start.24 = (pred[21]{0:T(512)(128)(4,1)S(1)}, pred[21]{0:T(512)(128)(4,1)}, u32[]{:S(2)}) copy-start(pred[21]{0:T(512)(128)(4,1)} %get-tuple-element.671) | copy-start | bytes 67
  1600.1 90.0 %copy-start.25 = (pred[21]{0:T(512)(128)(4,1)S(1)}, pred[21]{0:T(512)(128)(4,1)}, u32[]{:S(2)}) copy-start(pred[21]{0:T(512)(128)(4,1)} %broadcast_compare_fusion) | copy-start | bytes 67
  (15 other events, 98.3 us)
Sparse Core Ops, SparseCore 0:
  9.9 114.7 all-gather.10
  134.5 48.3 all-gather.12
  184.8 93.1 all-gather.14
  279.9 219.8 all-gather.18
  502.1 52.5 all-gather.16
  556.5 54.3 all-gather.20
  648.2 71.2 reduce-scatter.8
  723.4 71.2 reduce-scatter.6
  971.9 35.7 reduce-scatter.10
  1034.8 134.6 reduce-scatter.12
  1171.8 184.7 reduce-scatter.14
  1358.8 158.9 reduce-scatter.16
  1519.7 30.3 all-gather.22
  1551.9 28.3 all-gather.24
  1582.5 98.5 all-gather.26
where the time goes:
time: 1740 us; the launch traced here: 1730 us
  waiting for transfers between devices  1010 us (58%)
  matrix products  299 us (17%)
  blocking collectives  226 us (13%)
  local copies, waits for them, and re-layouts  112 us (6%)
  other arithmetic  59.6 us (3%)
    reduce_scatter x2, waiting for transfers between devices, reduce_rows(): lax.psum_scatter(blocks, ('grp', 'seq'), scatter_dimension=0, tiled=True)  266 us
    reduce_scatter x1, waiting for transfers between devices, local(): lax.psum_scatter(feed_grads, 'seq', scatter_dimension=0, tiled=True)  161 us
    all_gather x1, waiting for transfers between devices, local(): plane_tiles = lax.all_gather(weights_low, 'grp', axis=0, tiled=True)  116 us
    all_gather x1, waiting for transfers between devices, local(): feed_grads = lax.all_gather(feed_grads, 'grp', axis=0, tiled=True)  76.1 us
    all_gather x1, waiting for transfers between devices, local(): lax.all_gather(attn_weights, 'grp', axis=1, tiled=True)  73.6 us
    reduce_scatter x1, waiting for transfers between devices, local(): lax.psum_scatter(times_transpose(activated, down_weights).astype(jnp.bflo...  72.2 us
    reduce_scatter x1, waiting for transfers between devices, local(): lax.psum_scatter(times_transpose(gating_grad, gating_weights).astype(jnp....  59.5 us
    all_to_all x1, blocking collectives, local(): lax.all_to_all(head_context.reshape(-1, heads_here * HD).astype(jnp.bfloa...  59.3 us
  transfers between devices with their start and end apart: 17, of which 13 were waited for; matrix products, arithmetic and copies ran while one was open for 12% of the time, Pallas kernels for 0%

commit v1 on v0

--- a/solution.py
+++ b/solution.py
@@ -18,6 +18,29 @@
 ROPE_BASE = 10000.0
 MASKED = -1e30
 PRECISE = lax.Precision.HIGHEST
+
+
+def in_blocks(shard, dim, size):
+    shape = shard.shape
+    blocks = shard.reshape(*shape[:dim], size, shape[dim] // size, *shape[dim + 1 :])
+    return jnp.moveaxis(blocks, dim, 0)
+
+
+def joined_along(tiles, dim):
+    tiles = jnp.moveaxis(tiles, 0, dim)
+    dims = tiles.shape
+    return tiles.reshape(*dims[:dim], dims[dim] * dims[dim + 1], *dims[dim + 2 :])
+
+
+def pairwise_exchange(value, axis, split_dim, concat_dim):
+    peers, index = (lax.axis_size(axis), lax.axis_index(axis))
+    blocks = in_blocks(value, split_dim, peers)
+    gathered = [blocks[index]]
+    for step in range(1, peers):
+        sent = blocks[index ^ step]
+        gathered.append(lax.ppermute(sent, axis, [(i, i ^ step) for i in range(peers)]))
+    blocks = jnp.stack(gathered)[index ^ jnp.arange(peers)]
+    return joined_along(blocks, concat_dim)
 
 
 def rotate(values, positions, direction):
@@ -303,7 +326,7 @@
     turned_query = (
         rotate(head_query_grad, group_place, -1.0).reshape(-1, heads_here * HD).astype(jnp.bfloat16)
     )
-    query_grad = lax.all_to_all(turned_query, "seq", split_axis=0, concat_axis=1, tiled=True)
+    query_grad = pairwise_exchange(turned_query, "seq", 0, 1)
     key_part = rotate(key_part[:, None, :], group_place, -1.0)[:, 0, :]
     pair_grad = lax.psum_scatter(
         jnp.concatenate([key_part, value_part], axis=1), "seq", scatter_dimension=0, tiled=True

time: 1740 us -> 1740 us (level)
  blocking collectives: 226 us -> 185 us
  waiting for transfers between devices: 1010 us -> 1050 us
    all_to_all x1 -> x0, blocking collectives: 41.2 us -> none  [local(): lax.all_to_all(turned_query, 'seq', split_axis=0, concat_axis=1, tiled=True)]
    ppermute x0 -> x3, waiting for transfers between devices: none -> 30.3 us  [pairwise_exchange(): lax.ppermute(sent, axis, [(i, i ^ step) for i in range(peers)])]
  transfers between devices with their start and end apart: 17 -> 20, of which waited for: 13 -> 15; matrix products, arithmetic and copies ran while one was open for 12% -> 13% of each run, Pallas kernels for 0% -> 0%
where the time goes in v1:
time: 1740 us; the launch traced here: 1730 us
  waiting for transfers between devices  1050 us (60%)
  matrix products  299 us (17%)
  blocking collectives  185 us (11%)
  local copies, waits for them, and re-layouts  115 us (7%)
  other arithmetic  59.6 us (3%)
    reduce_scatter x2, waiting for transfers between devices, reduce_rows(): lax.psum_scatter(blocks, ('grp', 'seq'), scatter_dimension=0, tiled=True)  270 us
    reduce_scatter x1, waiting for transfers between devices, local(): lax.psum_scatter(feed_grads, 'seq', scatter_dimension=0, tiled=True)  161 us
    all_gather x1, waiting for transfers between devices, local(): plane_tiles = lax.all_gather(weights_low, 'grp', axis=0, tiled=True)  116 us
    all_gather x1, waiting for transfers between devices, local(): feed_grads = lax.all_gather(feed_grads, 'grp', axis=0, tiled=True)  76.3 us
    all_gather x1, waiting for transfers between devices, local(): lax.all_gather(attn_weights, 'grp', axis=1, tiled=True)  73.6 us
    reduce_scatter x1, waiting for transfers between devices, local(): lax.psum_scatter(times_transpose(activated, down_weights).astype(jnp.bflo...  72.2 us
    reduce_scatter x1, waiting for transfers between devices, local(): lax.psum_scatter(times_transpose(gating_grad, gating_weights).astype(jnp....  59.5 us
    all_to_all x1, blocking collectives, local(): lax.all_to_all(head_context.reshape(-1, heads_here * HD).astype(jnp.bfloa...  59.3 us
  transfers between devices with their start and end apart: 20, of which 15 were waited for; matrix products, arithmetic and copies ran while one was open for 13% of the time, Pallas kernels for 0%

profile of v1, /device:TPU:0, one launch (start us, length us, event | category | flops | bytes accessed | tf_op | source)
XLA Modules:
  0.0 1732.2 jit_solution(11586407400879836406)
XLA Ops:
  8.7 116.0 %all-gather.11.cloned.1.call-done = bf16[168,512,128]{2,1,0:T(8,128)(2,1)} async-done(((bf16[21,512,128]{2,1,0:T(8,128)(2,1)}), bf16[168,512,128]{2,1,0:T(8,128)(2,1)}) %all-gather.11.cloned.1.call-update) | async-done | bytes 22020112 | tf_op jit(solution)/shard_map/all_gather | solution.py:195
  134.4 48.4 %all-gather.13.cloned.1.call-done = bf16[4,64,4352]{2,1,0:T(8,128)(2,1)} async-done(((bf16[1,64,4352]{2,1,0:T(8,128)(2,1)}), bf16[4,64,4352]{2,1,0:T(8,128)(2,1)}) %all-gather.13.cloned.1.call-update) | async-done | bytes 2228240 | tf_op jit(solution)/shard_map/all_gather | solution.py:206
  204.3 73.6 %all-gather.15.cloned.1.call-done = bf16[4,512,4352]{2,1,0:T(8,128)(2,1)} async-done(((bf16[4,64,4352]{2,1,0:T(8,128)(2,1)}), bf16[4,512,4352]{2,1,0:T(8,128)(2,1)}) %all-gather.15.cloned.1.call-update) | async-done | bytes 17825808 | tf_op jit(solution)/shard_map/all_gather | solution.py:207
  296.3 40.8 %all-gather = s32[4,1,256]{2,1,0:T(1,128)S(1)} all-gather(s32[1,1,256]{2,1,0:T(1,128)} %bitcast.350), channel_id=1, replica_groups=mesh['grp'=8,'seq'=4] {'seq'}, dimensions={0}, use_global_device_ids=true | all-gather | bytes 5120 | tf_op jit(solution)/shard_map/all_gather | solution.py:236
  339.6 43.2 %all_gather.37 = bf16[1024,256]{0,1:T(8,128)(2,1)S(1)} all-gather(bf16[256,256]{0,1:T(8,128)(2,1)S(1)} %pad_maximum_fusion.12), channel_id=1, replica_groups=mesh['grp'=8,'seq'=4] {'seq'}, dimensions={0}, use_global_device_ids=true | all-gather | bytes 655360 | tf_op jit(solution)/shard_map/all_gather | solution.py:231
  388.0 17.3 while.36
  410.6 59.3 %all_to_all.45 = bf16[4,256,512]{2,1,0:T(8,128)(2,1)} all-to-all(bf16[4,256,512]{2,1,0:T(8,128)(2,1)} %convert_element_type.137), channel_id=1, replica_groups=mesh['grp'=8,'seq'=4] {'seq'}, dimensions={0} | all-to-all | bytes 2097152 | tf_op jit(solution)/shard_map/all_to_all | solution.py:246
  481.9 18.0 %all-gather.19.cloned.1.call-done = bf16[2048,2304]{0,1:T(8,128)(2,1)} async-done(((bf16[512,2304]{0,1:T(8,128)(2,1)}), bf16[2048,2304]{0,1:T(8,128)(2,1)}) %all-gather.19.cloned.1.call-update) | async-done | bytes 9437200 | tf_op jit(solution)/shard_map/all_gather | solution.py:214
  499.8 54.9 %all-gather.17.cloned.1.call-done = bf16[2048,2048]{1,0:T(8,128)(2,1)} async-done(((bf16[256,2048]{1,0:T(8,128)(2,1)}), bf16[2048,2048]{1,0:T(8,128)(2,1)}) %all-gather.17.cloned.1.call-update) | async-done | bytes 8388624 | tf_op jit(solution)/shard_map/all_gather | solution.py:257
  554.8 19.0 %fusion.95 = f32[2048,1536]{0,1:T(8,128)} fusion(bf16[2048,2048]{1,0:T(8,128)(2,1)} %all-gather.17.cloned.1.call-done, bf16[2048,2304]{0,1:T(8,128)(2,1)} %all-gather.19.cloned.1.call-done), kind=kOutput, calls=%fused_computation.135 | convolution fusion | flops 12884901888 | bytes 27262976 | tf_op jit(solution)/shard_map/dot_general | solution.py:260
  573.7 37.2 %all-gather.21.cloned.1.call-done = bf16[2048,2048]{1,0:T(8,128)(2,1)} async-done(((bf16[256,2048]{1,0:T(8,128)(2,1)}), bf16[2048,2048]{1,0:T(8,128)(2,1)}) %all-gather.21.cloned.1.call-update) | async-done | bytes 8388624 | tf_op jit(solution)/shard_map/all_gather | solution.py:215
  610.9 16.7 fusion.91
  629.3 18.8 %convolution_convert_fusion.3 = bf16[2048,2048]{1,0:T(8,128)(2,1)} fusion(bf16[2048,2304]{0,1:T(8,128)(2,1)} %all-gather.19.cloned.1.call-done, bf16[2048,768]{0,1:T(8,128)(2,1)} %get-tuple-element.680, bf16[2048,768]{0,1:T(8,128)(2,1)S(1)} %get-tuple-element.679), kind=kOutput, calls=%fused_computation.118 | convolution fusion | flops 12901679104 | bytes 20971520 | tf_op jit(solution)/shard_map/dot_general | solution.py:74
  648.1 11.9 convolution_convert_fusion.4
  660.0 59.5 %reduce-scatter.9.cloned.1.call-done = bf16[256,2048]{1,0:T(8,128)(2,1)} async-done(((bf16[2048,2048]{1,0:T(8,128)(2,1)}), bf16[256,2048]{1,0:T(8,128)(2,1)}) %reduce-scatter.9.cloned.1.call-update) | async-done | bytes 1048592 | tf_op jit(solution)/shard_map/reduce_scatter | solution.py:272
  722.5 72.2 %reduce-scatter.7.cloned.1.call-done = bf16[256,2048]{1,0:T(8,128)(2,1)} async-done(((bf16[2048,2048]{1,0:T(8,128)(2,1)}), bf16[256,2048]{1,0:T(8,128)(2,1)}) %reduce-scatter.7.cloned.1.call-update) | async-done | bytes 1048592 | tf_op jit(solution)/shard_map/reduce_scatter | solution.py:284
  811.2 25.8 %all-to-all-done.2 = bf16[256,4,512]{2,0,1:T(8,128)(2,1)} async-done(((bf16[256,4,512]{2,0,1:T(8,128)(2,1)}), bf16[256,4,512]{2,0,1:T(8,128)(2,1)}, u32[]{:S(2)}, u32[]{:S(2)}) %all-to-all-start.2) | async-done | bytes 1048608 | tf_op jit(solution)/shard_map/all_to_all | solution.py:302
  839.6 123.2 %while.37 = (s32[]{:T(128)}, f32[1024,128]{1,0:T(8,128)}, f32[1024,128]{1,0:T(8,128)}, f32[2,512,4,128]{3,1,0,2:T(8,128)}, s32[2,512]{1,0:T(2,128)S(1)}, /*index...) while((s32[]{:T(128)}, f32[1024,128]{1,0:T(8,128)}, ...), condition=%wide.region_11.12_spmd.clone.clone, body=%wide.region_9.11_spmd.clone.clone.sunk | while | flops 2742048256 | bytes 106783928 | solution.py:151
  850.4 22.8 %fusion.229 = f32[2,512,4,128]{3,1,0,2:T(8,128)} fusion(f32[2,512,4,128]{3,1,0,2:T(8,128)} %get-tuple-element.904, s32[]{:T(128)} %get-tuple-element.901, f32[512,4,1024]{2,0,1:T(8,128)} %fusion.224, f32[512,4,1024]{2,0,1:T(8,128)} %fusion.225, f32[4,512]{1,0:T(4,128)S(1)} %dynamic-slice_bitcast_fusion.5, pred[512,1024]{1,0:T(8,128)(4,1)} %fusion.226, ...), kind=kOutput, calls=%fused_computation.68.clone.1 | convolution fusion | flops 559942656 | bytes 35930624 | tf_op jit(solution)/shard_map/while/body/eval_jaxpr/hqk,kd->qhd/dot_general | solution.py:136
  873.2 21.1 %fusion.227 = f32[1024,128]{1,0:T(8,128)} fusion(f32[512,4,1024]{2,0,1:T(8,128)} %fusion.224, f32[512,4,1024]{2,0,1:T(8,128)} %fusion.225, f32[4,512]{1,0:T(4,128)S(1)} %dynamic-slice_bitcast_fusion.5, pred[512,1024]{1,0:T(8,128)(4,1)} %fusion.226, f32[1024,128]{1,0:T(8,128)} %get-tuple-element.902, ...), kind=kOutput, calls=%fused_computation.71.clone.1 | convolution fusion | flops 560204800 | bytes 36192768 | tf_op jit(solution)/shard_map/while/body/eval_jaxpr/hqk,qhd->kd/dot_general | solution.py:139
  911.9 22.8 %fusion.229 = f32[2,512,4,128]{3,1,0,2:T(8,128)} fusion(f32[2,512,4,128]{3,1,0,2:T(8,128)} %get-tuple-element.904, s32[]{:T(128)} %get-tuple-element.901, f32[512,4,1024]{2,0,1:T(8,128)} %fusion.224, f32[512,4,1024]{2,0,1:T(8,128)} %fusion.225, f32[4,512]{1,0:T(4,128)S(1)} %dynamic-slice_bitcast_fusion.5, pred[512,1024]{1,0:T(8,128)(4,1)} %fusion.226, ...), kind=kOutput, calls=%fused_computation.68.clone.1 | convolution fusion | flops 559942656 | bytes 35930624 | tf_op jit(solution)/shard_map/while/body/eval_jaxpr/hqk,kd->qhd/dot_general | solution.py:136
  934.7 21.2 %fusion.227 = f32[1024,128]{1,0:T(8,128)} fusion(f32[512,4,1024]{2,0,1:T(8,128)} %fusion.224, f32[512,4,1024]{2,0,1:T(8,128)} %fusion.225, f32[4,512]{1,0:T(4,128)S(1)} %dynamic-slice_bitcast_fusion.5, pred[512,1024]{1,0:T(8,128)(4,1)} %fusion.226, f32[1024,128]{1,0:T(8,128)} %get-tuple-element.902, ...), kind=kOutput, calls=%fused_computation.71.clone.1 | convolution fusion | flops 560204800 | bytes 36192768 | tf_op jit(solution)/shard_map/while/body/eval_jaxpr/hqk,qhd->kd/dot_general | solution.py:139
  982.8 23.7 %collective-permute-done = bf16[256,512]{1,0:T(8,128)(2,1)S(1)} collective-permute-done((bf16[256,512]{1,0:T(8,128)(2,1)S(1)}, bf16[256,512]{1,0:T(8,128)(2,1)S(1)}, u32[]{:S(2)}, u32[]{:S(2)}) %collective-permute-start) | collective-permute-done | bytes 262176 | tf_op jit(solution)/shard_map/ppermute | solution.py:41
  1059.2 15.9 convolution_convert_fusion.1
  1075.1 11.5 pad_maximum_fusion
  1086.6 83.4 %reduce-scatter.13.cloned.1.call-done = bf16[64,2304]{1,0:T(8,128)(2,1)} async-done(((bf16[2048,2304]{1,0:T(8,128)(2,1)}), bf16[64,2304]{1,0:T(8,128)(2,1)}) %reduce-scatter.13.cloned.1.call-update) | async-done | bytes 294928 | tf_op jit(solution)/shard_map/reduce_scatter | solution.py:311
  1170.1 187.1 %reduce-scatter.15.cloned.1.call-done = bf16[64,2048]{1,0:T(8,128)(2,1)} async-done(((bf16[2048,2048]{1,0:T(8,128)(2,1)}), bf16[64,2048]{1,0:T(8,128)(2,1)}) %reduce-scatter.15.cloned.1.call-update) | async-done | bytes 262160 | tf_op jit(solution)/shard_map/reduce_scatter | solution.py:311
  1357.2 161.1 %reduce-scatter.17.cloned.1.call-done = bf16[512,2304]{0,1:T(8,128)(2,1)} async-done(((bf16[2048,2304]{0,1:T(8,128)(2,1)}), bf16[512,2304]{0,1:T(8,128)(2,1)}) %reduce-scatter.17.cloned.1.call-update) | async-done | bytes 2359312 | tf_op jit(solution)/shard_map/reduce_scatter | solution.py:281
  1534.9 41.5 %psum.7 = f32[2,2048]{1,0:T(2,128)S(1)} all-reduce(f32[2,2048]{1,0:T(2,128)S(1)} %pad_maximum_fusion.13), channel_id=1, replica_groups=mesh['grp'=8,'seq'=4] {'grp','seq'}, use_global_device_ids=true, to_apply=%region_20.21 | all-reduce | flops 4096 | bytes 32768 | tf_op jit(solution)/shard_map/psum | solution.py:345
  1605.4 76.3 %all-gather.27.cloned.1.call-done = bf16[144,512,128]{2,1,0:T(8,128)(2,1)} async-done(((bf16[18,512,128]{2,1,0:T(8,128)(2,1)}), bf16[144,512,128]{2,1,0:T(8,128)(2,1)}) %all-gather.27.cloned.1.call-update) | async-done | bytes 18874384 | tf_op jit(solution)/shard_map/all_gather | solution.py:283
  1690.6 18.5 %fusion.97 = (f32[21,512,128]{2,1,0:T(8,128)}, f32[21,512,128]{2,1,0:T(8,128)}) fusion(f32[21,512,128]{2,1,0:T(8,128)} %param.24, f32[21,512,128]{2,1,0:T(8,128)} %param.23, f32[21,128,128]{2,1,0:T(8,128)S(1)} %copy-done, f32[21,512,512]{2,1,0:T(8,128)} %param.25, bf16[21,512,128]{2,1,0:T(8,128)(2,1)} %gather_fusion.4, ...), kind=kOutput, calls=%fused_computation.137 | convolution fusion | flops 1772617728 | bytes 50921512 | tf_op jit(solution)/shard_map/zic,zcd->zid/dot_general | solution.py:367
  1709.1 16.1 multiply_subtract_fusion
  (245 shorter events, 279.0 us)
Async XLA Ops:
  7.2 1683.4 %copy-start = (f32[21,128,128]{2,1,0:T(8,128)S(1)}, f32[21,128,128]{2,1,0:T(8,128)}, u32[]{:S(2)}) copy-start(f32[21,128,128]{2,1,0:T(8,128)} %param.26) | copy-start | bytes 4128772
  7.2 117.5 %all-gather.11.cloned.1.call-start = ((), (), s32[]{:S(2)}) async-start(), calls=%async_computation.9 | async-start | bytes 24772608 | tf_op jit(solution)/shard_map/all_gather | solution.py:195
  7.9 174.9 %all-gather.13.cloned.1.call-start = ((), (), s32[]{:S(2)}) async-start(), calls=%async_computation.10 | async-start | bytes 2785280 | tf_op jit(solution)/shard_map/all_gather | solution.py:206
  8.7 174.5 %copy-start.1 = (s32[166]{0:T(256)S(1)}, s32[166]{0:T(256)}, u32[]{:S(2)}) copy-start(s32[166]{0:T(256)} %param.20) | copy-start | bytes 1996
  8.7 175.3 %copy-start.7 = (bf16[256,2048]{1,0:T(8,128)(2,1)S(1)}, bf16[256,2048]{1,0:T(8,128)(2,1)}, u32[]{:S(2)}) copy-start(bf16[256,2048]{1,0:T(8,128)(2,1)} %param.17) | copy-start | bytes 3145732
  134.4 143.5 %all-gather.15.cloned.1.call-start = ((), (), s32[]{:S(2)}) async-start(), calls=%async_computation.11 | async-start | bytes 20054016 | tf_op jit(solution)/shard_map/all_gather | solution.py:207
  182.9 317.0 %all-gather.19.cloned.1.call-start = ((), (), s32[]{:S(2)}) async-start(), calls=%async_computation.13 | async-start | bytes 11796480 | tf_op jit(solution)/shard_map/all_gather | solution.py:214
  202.7 136.5 %copy-start.22 = (f32[64]{0:T(128)}, f32[64]{0:T(128)S(1)}, u32[]{:S(2)}) copy-start(f32[64]{0:T(128)S(1)} %multiply_power_fusion) | copy-start | bytes 772
  203.3 80.9 %copy-start.19 = (f32[256]{0:T(256)}, f32[256]{0:T(256)S(1)}, u32[]{:S(2)}) copy-start(f32[256]{0:T(256)S(1)} %get-tuple-element.707) | copy-start | bytes 3076
  204.3 80.0 %copy-start.13 = (f32[1,2048]{1,0:T(1,128)}, f32[1,2048]{1,0:T(1,128)S(1)}, u32[]{:S(2)}) copy-start(f32[1,2048]{1,0:T(1,128)S(1)} %get-tuple-element.701) | copy-start | bytes 24580
  291.7 91.5 %all-to-all-start = ((bf16[256,4,512]{0,2,1:T(8,128)(2,1)}), bf16[256,4,512]{0,2,1:T(8,128)(2,1)S(1)}, u32[]{:S(2)}, u32[]{:S(2)}) async-start(bf16[256,4,512]{0,2,1:T(8,128)(2,1)} %bitcast.5), calls=%async_computation | async-start | bytes 2097152 | tf_op jit(solution)/shard_map/all_to_all | solution.py:240
  296.3 258.4 %all-gather.17.cloned.1.call-start = ((), (), s32[]{:S(2)}) async-start(), calls=%async_computation.12 | async-start | bytes 9437184 | tf_op jit(solution)/shard_map/all_gather | solution.py:257
  481.1 129.8 %all-gather.21.cloned.1.call-start = ((), (), s32[]{:S(2)}) async-start(), calls=%async_computation.15 | async-start | bytes 9437184 | tf_op jit(solution)/shard_map/all_gather | solution.py:215
  481.7 237.8 %reduce-scatter.9.cloned.1.call-start = ((), (), s32[]{:S(2)}) async-start(), calls=%async_computation.16 | async-start | bytes 9437184 | tf_op jit(solution)/shard_map/reduce_scatter | solution.py:272
  648.1 146.6 %reduce-scatter.7.cloned.1.call-start = ((), (), s32[]{:S(2)}) async-start(), calls=%async_computation.14 | async-start | bytes 9437184 | tf_op jit(solution)/shard_map/reduce_scatter | solution.py:284
  806.5 30.4 %all-to-all-start.2 = ((bf16[256,4,512]{2,0,1:T(8,128)(2,1)}), bf16[256,4,512]{2,0,1:T(8,128)(2,1)}, u32[]{:S(2)}, u32[]{:S(2)}) async-start(bf16[256,4,512]{2,0,1:T(8,128)(2,1)} %bitcast.324), calls=%async_computation.4 | async-start | bytes 2097152 | tf_op jit(solution)/shard_map/all_to_all | solution.py:302
  811.1 205.2 %reduce-scatter.11.cloned.1.call-start = ((), (), s32[]{:S(2)}) async-start(), calls=%async_computation.17 | async-start | bytes 1310720 | tf_op jit(solution)/shard_map/reduce_scatter | solution.py:331
  839.6 127.5 %copy-start.23 = (f32[64]{0:T(128)S(1)}, f32[64]{0:T(128)}, u32[]{:S(2)}) copy-start(f32[64]{0:T(128)} %copy-done.22) | copy-start | bytes 772
  971.5 198.5 %reduce-scatter.13.cloned.1.call-start = ((), (), s32[]{:S(2)}) async-start(), calls=%async_computation.18 | async-start | bytes 9732096 | tf_op jit(solution)/shard_map/reduce_scatter | solution.py:311
  978.4 28.2 %collective-permute-start = (bf16[256,512]{1,0:T(8,128)(2,1)S(1)}, bf16[256,512]{1,0:T(8,128)(2,1)S(1)}, u32[]{:S(2)}, u32[]{:S(2)}) collective-permute-start(bf16[256,512]{1,0:T(8,128)(2,1)S(1)} %get-tuple-element.693), channel_id=1, source_target_pairs={{0,1},{1,0},{2,3},{3,2},{4,5},{5,4},{6,7},{7,6},{8,9},{9,8},{10,11... | collective-permute-start | bytes 786440 | tf_op jit(solution)/shard_map/ppermute | solution.py:41
  978.4 28.1 %collective-permute-start.1 = (bf16[256,512]{1,0:T(8,128)(2,1)S(1)}, bf16[256,512]{1,0:T(8,128)(2,1)S(1)}, u32[]{:S(2)}, u32[]{:S(2)}) collective-permute-start(bf16[256,512]{1,0:T(8,128)(2,1)S(1)} %get-tuple-element.692), channel_id=1, source_target_pairs={{0,2},{1,3},{2,0},{3,1},{4,6},{5,7},{6,4},{7,5},{8,10},{9,11},{10,... | collective-permute-start | bytes 786440 | tf_op jit(solution)/shard_map/ppermute | solution.py:41
  980.4 32.7 %collective-permute-start.2 = (bf16[256,512]{1,0:T(8,128)(2,1)S(1)}, bf16[256,512]{1,0:T(8,128)(2,1)S(1)}, u32[]{:S(2)}, u32[]{:S(2)}) collective-permute-start(bf16[256,512]{1,0:T(8,128)(2,1)S(1)} %get-tuple-element.691), channel_id=1, source_target_pairs={{0,3},{1,2},{2,1},{3,0},{4,7},{5,6},{6,5},{7,4},{8,11},{9,10},{10,... | collective-permute-start | bytes 786440 | tf_op jit(solution)/shard_map/ppermute | solution.py:41
  1031.2 326.0 %reduce-scatter.15.cloned.1.call-start = ((), (), s32[]{:S(2)}) async-start(), calls=%async_computation.20 | async-start | bytes 8650752 | tf_op jit(solution)/shard_map/reduce_scatter | solution.py:311
  1048.3 470.0 %reduce-scatter.17.cloned.1.call-start = ((), (), s32[]{:S(2)}) async-start(), calls=%async_computation.22 | async-start | bytes 11796480 | tf_op jit(solution)/shard_map/reduce_scatter | solution.py:281
  1086.6 436.1 %copy-start.2 = (s32[166]{0:T(256)S(1)}, s32[166]{0:T(256)}, u32[]{:S(2)}) copy-start(s32[166]{0:T(256)} %param.20) | copy-start | bytes 1996
  1086.6 495.8 %all-gather.23.cloned.1.call-start = ((), (), s32[]{:S(2)}) async-start(), calls=%async_computation.19 | async-start | bytes 2654208 | tf_op jit(solution)/shard_map/all_gather | solution.py:312
  1170.0 412.4 %all-gather.25.cloned.1.call-start = ((), (), s32[]{:S(2)}) async-start(), calls=%async_computation.21 | async-start | bytes 2359296 | tf_op jit(solution)/shard_map/all_gather | solution.py:312
  1357.2 324.5 %all-gather.27.cloned.1.call-start = ((), (), s32[]{:S(2)}) async-start(), calls=%async_computation.23 | async-start | bytes 21233664 | tf_op jit(solution)/shard_map/all_gather | solution.py:283
  1525.6 51.6 %copy-start.16 = (f32[2,2048]{1,0:T(2,128)S(1)}, f32[2,2048]{1,0:T(2,128)}, u32[]{:S(2)}) copy-start(f32[2,2048]{1,0:T(2,128)} %param.27) | copy-start | bytes 49156
  1525.6 51.6 %copy-start.21 = (f32[2,2048]{1,0:T(2,128)S(1)}, f32[2,2048]{1,0:T(2,128)}, u32[]{:S(2)}) copy-start(f32[2,2048]{1,0:T(2,128)} %param.28) | copy-start | bytes 49156
  1600.4 90.2 %copy-start.24 = (pred[21]{0:T(512)(128)(4,1)S(1)}, pred[21]{0:T(512)(128)(4,1)}, u32[]{:S(2)}) copy-start(pred[21]{0:T(512)(128)(4,1)} %get-tuple-element.671) | copy-start | bytes 67
  1600.4 90.2 %copy-start.25 = (pred[21]{0:T(512)(128)(4,1)S(1)}, pred[21]{0:T(512)(128)(4,1)}, u32[]{:S(2)}) copy-start(pred[21]{0:T(512)(128)(4,1)} %broadcast_compare_fusion) | copy-start | bytes 67
  (18 other events, 221.0 us)
Sparse Core Ops, SparseCore 0:
  9.9 114.7 all-gather.10
  134.5 48.3 all-gather.12
  184.8 93.1 all-gather.14
  279.9 219.8 all-gather.18
  502.1 52.5 all-gather.16
  556.5 54.3 all-gather.20
  648.2 71.2 reduce-scatter.8
  723.4 71.2 reduce-scatter.6
  971.7 40.6 reduce-scatter.10
  1031.3 138.6 reduce-scatter.12
  1172.3 184.8 reduce-scatter.14
  1359.4 158.9 reduce-scatter.16
  1520.3 30.3 all-gather.22
  1552.4 28.3 all-gather.24
  1583.1 98.5 all-gather.26
